TPU v7x, 32 devices: a whole 2x2x4 slice. The times are simulated.
32 devices in a mesh: prow: 8 (over z, x), pcol: 4 (over y, core).
Axes of the slice: x: 2, y: 2, z: 4, core: 2. Of those that a mesh axis runs over, the one named last changes fastest.
Arguments:
- sigma_top: bfloat16 [8, 8, 128, 128], P('prow', 'pcol'), may hold values from -6 to 6
- factor_one: bfloat16 [8, 8, 128, 128], P('prow', 'pcol'), may hold values from -0.1875 to 0.1875
- inverse_one: bfloat16 [8, 128, 128], P('prow'), may hold values from -0.5 to 0.5
- pattern_one: int32 [8, 8], replicated, may hold values from 0 to 7, as said below
- factor_two: bfloat16 [8, 8, 128, 128], P('prow', 'pcol'), may hold values from -0.25 to 0.25
- parent_block: bfloat16 [8, 128, 128], P('prow'), may hold values from -0.25 to 0.25
- inverse_two: bfloat16 [8, 128, 128], P('prow'), may hold values from -0.5 to 0.5
- parent_two: int32 [8], replicated, may hold values from 0 to 7
- keep_two: int32 [8, 8], replicated, may hold values 0 or 1
Outputs:
- inverse_top_one: bfloat16 [8, 8, 128, 128], P('prow')
- diag_one: float32 [8, 128, 128], P('prow')
- inverse_top_two: bfloat16 [8, 8, 128, 128], P('prow')
- inverse_parent_two: float32 [8, 128, 128], P('prow')
- diag_two: float32 [8, 128, 128], P('prow')
Inputs may be any that keep to these rules, and one draw needn't show every extreme that they name: Each row of pattern_one lists 8 distinct block rows of the top region. keep_two[i, k] = 1 where level-two supernode i's pattern holds the k-th tile of its parent's pattern. parent_two names level-one supernodes.
All inputs are finite; a program needn't handle non-finite values.
Results may differ from a plain program's by a relative error of at most 0.023.
Values may be sent and summed in bfloat16 or wider, within the bound.
A program may use at most 64 MiB of HBM per device.

v0:
```python
import jax
import jax.numpy as jnp
from jax import lax
from jax.sharding import PartitionSpec as P

highest = lax.Precision.HIGHEST


def split_product(form, left, right):
    upper_part = right.astype(jnp.bfloat16)
    lower_part = (right - upper_part.astype(jnp.float32)).astype(jnp.bfloat16)
    first = jnp.einsum(form, left, upper_part, preferred_element_type=jnp.float32)
    return first + jnp.einsum(form, left, lower_part, preferred_element_type=jnp.float32)


def body(
    sigma_top,
    factor_one,
    inverse_one,
    pattern_one,
    factor_two,
    parent_block,
    inverse_two,
    parent_two,
    keep_two,
):
    rows_here = sigma_top.shape[0]
    cols_here = sigma_top.shape[1]
    tile_width = sigma_top.shape[2]
    prow_index = lax.axis_index("prow")
    pcol_index = lax.axis_index("pcol")
    first_row = prow_index * rows_here
    column_ids = pcol_index * cols_here + jnp.arange(cols_here, dtype=jnp.int32)
    top_rows = first_row + jnp.arange(rows_here, dtype=jnp.int32)
    owner_column = first_row // cols_here
    diagonal_owner = owner_column == pcol_index
    offset = jnp.clip(first_row - pcol_index * cols_here, 0, cols_here - rows_here)
    total_one = pattern_one.shape[0]
    local_one = factor_one.shape[0]
    lower_one = jnp.tril(inverse_one)
    scaled_local = jnp.einsum(
        "jkwv,jvx->jkwx", factor_one, lower_one, preferred_element_type=jnp.float32
    ).astype(jnp.bfloat16)
    scaled_rows = lax.all_gather(scaled_local, "pcol", axis=1, tiled=True)
    own_pattern = lax.dynamic_slice_in_dim(pattern_one, prow_index * local_one, local_one, 0)
    picker_one = (own_pattern[:, :, None] == column_ids[None, None, :]).astype(jnp.bfloat16)
    spread_one = jnp.einsum(
        "jkc,jkwv->jcwv", picker_one, scaled_rows, preferred_element_type=jnp.float32
    ).astype(jnp.bfloat16)
    spread_all = lax.all_gather(spread_one, "prow", axis=0, tiled=True)
    partial_one = jnp.einsum(
        "acwv,jcvx->ajwx", sigma_top, spread_all, preferred_element_type=jnp.float32
    )
    summed_one = lax.psum(partial_one.astype(jnp.bfloat16), "pcol").astype(jnp.float32)
    member_one = jnp.sum(
        (pattern_one[None, :, :] == top_rows[:, None, None]).astype(jnp.float32), axis=2
    )
    inverse_top_one = (-summed_one * member_one[:, :, None, None]).astype(jnp.bfloat16)
    own_rows = lax.dynamic_slice_in_dim(spread_all, offset, rows_here, 1)
    quadratic_one = split_product("jawv,ajwx->jvx", own_rows, summed_one)
    quadratic_one = jnp.where(diagonal_owner, quadratic_one, 0.0)
    lower_float = lower_one.astype(jnp.float32)
    gram_one = jnp.einsum("jwv,jwx->jvx", lower_float, lower_float, precision=highest)
    placed = lax.dynamic_update_slice_in_dim(
        jnp.zeros((total_one, tile_width, tile_width), jnp.float32),
        gram_one,
        prow_index * local_one,
        0,
    )
    partial_diag = quadratic_one + jnp.where(pcol_index == 0, placed, 0.0)
    diagonal_all = lax.psum(partial_diag, ("prow", "pcol"))
    diag_one = lax.dynamic_slice_in_dim(diagonal_all, prow_index * local_one, local_one, 0)
    local_two = factor_two.shape[0]
    lower_two = jnp.tril(inverse_two)
    scaled_two = jnp.einsum(
        "ikwv,ivx->ikwx", factor_two, lower_two, preferred_element_type=jnp.float32
    ).astype(jnp.bfloat16)
    scaled_parent = jnp.einsum(
        "iwv,ivx->iwx", parent_block, lower_two, preferred_element_type=jnp.float32
    ).astype(jnp.bfloat16)
    scaled_rows_two = lax.all_gather(scaled_two, "pcol", axis=1, tiled=True)
    parent_hot = (parent_two[:, None] == jnp.arange(total_one, dtype=jnp.int32)[None, :]).astype(
        jnp.int32
    )
    parent_pattern = jnp.sum(parent_hot[:, :, None] * pattern_one[None, :, :], axis=1)
    own_parent_pattern = lax.dynamic_slice_in_dim(
        parent_pattern, prow_index * local_two, local_two, 0
    )
    own_keep = lax.dynamic_slice_in_dim(keep_two, prow_index * local_two, local_two, 0)
    picker_two = (
        (own_parent_pattern[:, :, None] == column_ids[None, None, :]).astype(jnp.int32)
        * own_keep[:, :, None]
    ).astype(jnp.bfloat16)
    spread_two = jnp.einsum(
        "ikc,ikwv->icwv", picker_two, scaled_rows_two, preferred_element_type=jnp.float32
    ).astype(jnp.bfloat16)
    spread_all_two, parent_all = (
        lax.all_gather(spread_two, "prow", axis=0, tiled=True),
        lax.all_gather(scaled_parent, "prow", axis=0, tiled=True),
    )
    partial_two = jnp.einsum(
        "acwv,icvx->aiwx", sigma_top, spread_all_two, preferred_element_type=jnp.float32
    )
    inherited = jnp.einsum(
        "ij,ajwv->aiwv",
        parent_hot.astype(jnp.bfloat16),
        inverse_top_one,
        preferred_element_type=jnp.float32,
    ).astype(jnp.bfloat16)
    carried_rows = jnp.einsum(
        "aiwv,ivx->aiwx", inherited, parent_all, preferred_element_type=jnp.float32
    )
    partial_two = partial_two + jnp.where(diagonal_owner, carried_rows, 0.0)
    summed_two = lax.psum(partial_two.astype(jnp.bfloat16), "pcol").astype(jnp.float32)
    member_two = jnp.sum(
        (parent_pattern[None, :, :] == top_rows[:, None, None]).astype(jnp.float32)
        * keep_two[None, :, :].astype(jnp.float32),
        axis=2,
    )
    inverse_top_two = (-summed_two * member_two[:, :, None, None]).astype(jnp.bfloat16)
    own_two = lax.dynamic_slice_in_dim(spread_all_two, offset, rows_here, 1)
    cross = jnp.einsum("aiwv,iawx->ivx", inherited, own_two, preferred_element_type=jnp.float32)
    quadratic_two = split_product("iawv,aiwx->ivx", own_two, summed_two)
    cross = jnp.where(diagonal_owner, cross, 0.0)
    quadratic_two = jnp.where(diagonal_owner, quadratic_two, 0.0)
    cross_part, quadratic_part = (
        lax.psum_scatter(
            cross.astype(jnp.bfloat16), "prow", scatter_dimension=0, tiled=True
        ).astype(jnp.float32),
        lax.psum_scatter(
            quadratic_two.astype(jnp.bfloat16), "prow", scatter_dimension=0, tiled=True
        ).astype(jnp.float32),
    )
    cross_sum, quadratic_sum = (
        lax.psum(cross_part.astype(jnp.bfloat16), "pcol").astype(jnp.float32),
        lax.psum(quadratic_part.astype(jnp.bfloat16), "pcol").astype(jnp.float32),
    )
    own_hot = lax.dynamic_slice_in_dim(parent_hot, prow_index * local_two, local_two, 0).astype(
        jnp.float32
    )
    parent_diag = jnp.einsum("ij,jwv->iwv", own_hot, diagonal_all, precision=highest)
    parent_float = scaled_parent.astype(jnp.float32)
    carried = cross_sum + jnp.einsum("iwv,ivx->iwx", parent_diag, parent_float, precision=highest)
    lower_two_float = lower_two.astype(jnp.float32)
    diag_two = jnp.einsum("iwv,iwx->ivx", lower_two_float, lower_two_float, precision=highest)
    diag_two = (
        diag_two
        + quadratic_sum
        + jnp.einsum("iwv,iwx->ivx", parent_float, carried, precision=highest)
    )
    return (inverse_top_one, diag_one, inverse_top_two, -carried, diag_two)


def solution(mesh):
    in_specs = (
        P("prow", "pcol", None, None),
        P("prow", "pcol", None, None),
        P("prow", None, None),
        P(),
        P("prow", "pcol", None, None),
        P("prow", None, None),
        P("prow", None, None),
        P(),
        P(),
    )
    out_specs = (
        P("prow", None, None, None),
        P("prow", None, None),
        P("prow", None, None, None),
        P("prow", None, None),
        P("prow", None, None),
    )
    return jax.shard_map(body, mesh=mesh, in_specs=in_specs, out_specs=out_specs, check_vma=False)
```

profile of v0, /device:TPU:0, one launch (start us, length us, event | category | flops | bytes accessed | tf_op | source)
XLA Modules:
  0.0 453.0 jit_solution(8151209483114322396)
XLA Ops:
  7.2 1.1 fusion.10
  8.4 7.2 %all-gather = bf16[8,128,128]{2,1,0:T(8,128)(2,1)S(1)} all-gather(bf16[2,128,128]{2,1,0:T(8,128)(2,1)S(1)} %copy.72), channel_id=2, replica_groups=mesh['prow'=8,'pcol'=4] {'pcol'}, dimensions={0}, use_global_device_ids=true | all-gather | bytes 327680 | tf_op jit(solution)/shard_map/all_gather | solution.py:44
  16.0 31.9 %all-gather.1 = bf16[16,128,128]{2,1,0:T(8,128)(2,1)S(1)} all-gather(bf16[2,128,128]{2,1,0:T(8,128)(2,1)S(1)} %copy.74), channel_id=3, replica_groups=mesh['prow'=8,'pcol'=4] {'prow'}, dimensions={0}, use_global_device_ids=true | all-gather | bytes 589824 | tf_op jit(solution)/shard_map/all_gather | solution.py:50
  47.9 1.1 fusion.7
  50.9 5.8 %all-gather.2 = bf16[8,128,128]{2,1,0:T(8,128)(2,1)S(1)} all-gather(bf16[2,128,128]{2,1,0:T(8,128)(2,1)S(1)} %copy.79), channel_id=4, replica_groups=mesh['prow'=8,'pcol'=4] {'pcol'}, dimensions={0}, use_global_device_ids=true | all-gather | bytes 327680 | tf_op jit(solution)/shard_map/all_gather | solution.py:81
  57.0 31.5 %all-gather.3 = bf16[16,128,128]{2,1,0:T(8,128)(2,1)S(1)} all-gather(bf16[2,128,128]{2,1,0:T(8,128)(2,1)S(1)} %copy.81), channel_id=5, replica_groups=mesh['prow'=8,'pcol'=4] {'prow'}, dimensions={0}, use_global_device_ids=true | all-gather | bytes 589824 | tf_op jit(solution)/shard_map/all_gather | solution.py:98
  88.7 26.4 %all-gather.4 = bf16[1024,128]{0,1:T(8,128)(2,1)S(1)} all-gather(bf16[128,128]{0,1:T(8,128)(2,1)S(1)} %bitcast.162), channel_id=6, replica_groups=mesh['prow'=8,'pcol'=4] {'prow'}, dimensions={0}, use_global_device_ids=true | all-gather | bytes 294912 | tf_op jit(solution)/shard_map/all_gather | solution.py:99
  115.5 1.1 fusion.112
  117.2 0.9 fusion.9
  118.2 0.9 copy-done.1
  121.5 1.0 fusion.6
  122.7 26.8 %all-reduce.10.cloned.1.call-done = bf16[1,8,128,128]{2,3,1,0:T(8,128)(2,1)} async-done(((bf16[1,8,128,128]{2,3,1,0:T(8,128)(2,1)}), bf16[1,8,128,128]{2,3,1,0:T(8,128)(2,1)}) %all-reduce.10.cloned.1.call-update) | async-done | bytes 262160 | tf_op jit(solution)/shard_map/psum | solution.py:114
  149.5 1.3 fusion.32
  150.9 1.0 fusion.3
  152.1 0.9 copy.92
  153.0 0.9 copy.93
  153.9 128.7 %all-reduce.8.cloned.1.call-done = f32[8,128,128]{2,1,0:T(8,128)} async-done(((f32[8,128,128]{2,1,0:T(8,128)}), f32[8,128,128]{2,1,0:T(8,128)}) %all-reduce.8.cloned.1.call-update) | async-done | bytes 524304 | tf_op jit(solution)/shard_map/psum | solution.py:71
  282.6 1.8 fusion.24
  284.5 61.9 %reduce-scatter.3.cloned.1.call-done = bf16[1,128,128]{2,1,0:T(8,128)(2,1)} async-done(((bf16[8,128,128]{2,1,0:T(8,128)(2,1)}), bf16[1,128,128]{2,1,0:T(8,128)(2,1)}) %reduce-scatter.3.cloned.1.call-update) | async-done | bytes 32784 | tf_op jit(solution)/shard_map/reduce_scatter | solution.py:127
  346.4 63.8 %reduce-scatter.5.cloned.1.call-done = bf16[1,128,128]{2,1,0:T(8,128)(2,1)} async-done(((bf16[8,128,128]{2,1,0:T(8,128)(2,1)}), bf16[1,128,128]{2,1,0:T(8,128)(2,1)}) %reduce-scatter.5.cloned.1.call-update) | async-done | bytes 32784 | tf_op jit(solution)/shard_map/reduce_scatter | solution.py:130
  410.3 1.5 constant_dynamic-slice_fusion.3
  411.8 31.2 %all-reduce.12.cloned.1.call-done = (bf16[1,128,128]{2,1,0:T(8,128)(2,1)}, bf16[1,128,128]{2,1,0:T(8,128)(2,1)}) async-done(((bf16[1,128,128]{2,1,0:T(8,128)(2,1)}, bf16[1,128,128]{2,1,0:T(8,128)(2,1)}), (bf16[1,128,128]{2,1,0:T(8,128)(2,1)}, bf16[1,128,128]{2,1,0:T(8,128)(2,1)})) %all-reduce.12.cloned.1.call-update) | async-done | bytes 65552 | tf_op jit(solution)/shard_map/psum | solution.py:135
  442.9 1.6 fusion.102
  445.3 0.8 fusion.15
  (64 shorter events, 7.6 us)
Async XLA Ops:
  7.2 40.7 %copy-start = (bf16[1,2,128,128]{3,2,1,0:T(8,128)(2,1)S(1)}, bf16[1,2,128,128]{3,2,1,0:T(8,128)(2,1)}, u32[]{:S(2)}) copy-start(bf16[1,2,128,128]{3,2,1,0:T(8,128)(2,1)} %param.9) | copy-start | bytes 196612
  7.2 108.3 %all-reduce.6.cloned.1.call-start = ((), (), s32[]{:S(2)}) async-start(), calls=%async_computation.2 | async-start | bytes 524288 | tf_op jit(solution)/shard_map/psum | solution.py:54
  8.4 7.2 %copy-start.9 = (s32[8,8]{1,0:T(8,128)S(1)}, s32[8,8]{1,0:T(8,128)}, u32[]{:S(2)}) copy-start(s32[8,8]{1,0:T(8,128)} %param.12) | copy-start | bytes 772
  48.9 100.6 %all-reduce.10.cloned.1.call-start = ((), (), s32[]{:S(2)}) async-start(), calls=%async_computation.4 | async-start | bytes 524288 | tf_op jit(solution)/shard_map/psum | solution.py:114
  49.1 0.7 copy-start.11
  49.1 1.4 copy-start.6
  49.4 1.1 copy-start.4
  49.8 0.7 copy-start.10
  57.0 31.5 %copy-start.7 = (bf16[1,128,128]{2,1,0:T(8,128)(2,1)S(1)}, bf16[1,128,128]{2,1,0:T(8,128)(2,1)}, u32[]{:S(2)}) copy-start(bf16[1,128,128]{2,1,0:T(8,128)(2,1)} %param.14) | copy-start | bytes 98308
  118.2 0.9 copy-start.1
  118.2 164.4 %all-reduce.8.cloned.1.call-start = ((), (), s32[]{:S(2)}) async-start(), calls=%async_computation.3 | async-start | bytes 1048576 | tf_op jit(solution)/shard_map/psum | solution.py:71
  119.4 0.8 copy-start.5
  120.4 0.8 copy-start.2
  121.2 225.2 %reduce-scatter.3.cloned.1.call-start = ((), (), s32[]{:S(2)}) async-start(), calls=%async_computation.5 | async-start | bytes 294912 | tf_op jit(solution)/shard_map/reduce_scatter | solution.py:127
  122.6 287.7 %reduce-scatter.5.cloned.1.call-start = ((), (), s32[]{:S(2)}) async-start(), calls=%async_computation.6 | async-start | bytes 294912 | tf_op jit(solution)/shard_map/reduce_scatter | solution.py:130
  149.5 1.3 copy-start.3
  151.9 291.0 %all-reduce.12.cloned.1.call-start = ((), (), s32[]{:S(2)}) async-start(), calls=%async_computation.7 | async-start | bytes 131072 | tf_op jit(solution)/shard_map/psum | solution.py:135
  444.5 0.8 copy-start.8
Sparse Core Ops, SparseCore 0:
  49.1 32.7 all-reduce.5
  118.3 31.1 all-reduce.9
  154.8 127.7 all-reduce.7
  286.2 60.2 reduce-scatter.2
  350.0 60.2 reduce-scatter.4
  412.6 30.2 all-reduce.11
where the time goes:
time: 454 us; the launch traced here: 453 us
  waiting for transfers between devices  313 us (69%)
  blocking collectives  103 us (23%)
  between operations  14.4 us (3%)
  matrix products  13.2 us (3%)
  local copies, waits for them, and re-layouts  8.08 us (2%)
    psum x1, waiting for transfers between devices, body(): diagonal_all = lax.psum(partial_diag, ('prow', 'pcol'))  129 us
    reduce_scatter x1, waiting for transfers between devices, body(): lax.psum_scatter(quadratic_two.astype(jnp.bfloat16), 'prow', scatter_dime...  63.8 us
    reduce_scatter x1, waiting for transfers between devices, body(): lax.psum_scatter(cross.astype(jnp.bfloat16), 'prow', scatter_dimension=0,...  61.9 us
    all_gather x1, blocking collectives, body(): spread_all = lax.all_gather(spread_one, 'prow', axis=0, tiled=True)  31.9 us
    all_gather x1, blocking collectives, body(): lax.all_gather(spread_two, 'prow', axis=0, tiled=True)  31.5 us
    psum x1, waiting for transfers between devices, body(): lax.psum(cross_part.astype(jnp.bfloat16), 'pcol').astype(jnp.float32)  31.2 us
    psum x1, waiting for transfers between devices, body(): lax.psum(partial_two.astype(jnp.bfloat16), 'pcol').astype(jnp.float32)  26.8 us
    all_gather x1, blocking collectives, body(): lax.all_gather(scaled_parent, 'prow', axis=0, tiled=True)  26.4 us
  transfers between devices with their start and end apart: 6, of which 5 were waited for; matrix products, arithmetic and copies ran while one was open for 3% of the time, Pallas kernels for 0%

commit v1 on v0

--- a/solution.py
+++ b/solution.py
@@ -132,7 +132,7 @@
         ).astype(jnp.float32),
     )
     cross_sum, quadratic_sum = (
-        lax.psum(cross_part.astype(jnp.bfloat16), "pcol").astype(jnp.float32),
+        jnp.sum(lax.all_gather(cross_part.astype(jnp.bfloat16), "pcol"), 0).astype(jnp.float32),
         lax.psum(quadratic_part.astype(jnp.bfloat16), "pcol").astype(jnp.float32),
     )
     own_hot = lax.dynamic_slice_in_dim(parent_hot, prow_index * local_two, local_two, 0).astype(

time: 454 us -> 429 us (0.945)
  waiting for transfers between devices: 313 us -> 274 us
  blocking collectives: 103 us -> 119 us
    psum x1 -> x0, waiting for transfers between devices: 31.2 us -> none  [body(): lax.psum(cross_part.astype(jnp.bfloat16), 'pcol').astype(jnp.float32)]
    psum x0 -> x1, blocking collectives: none -> 10.8 us  [body(): lax.psum(quadratic_part.astype(jnp.bfloat16), 'pcol').astype(jnp.float32)]
    reduce_scatter x1, waiting for transfers between devices: 63.8 us -> 57.2 us  [body(): lax.psum_scatter(quadratic_two.astype(jnp.bfloat16), 'prow', scatter_dime...]
    all_gather x0 -> x1, blocking collectives: none -> 5.62 us  [body(): lax.all_gather(cross_part.astype(jnp.bfloat16), 'pcol')]
  transfers between devices with their start and end apart: 6 -> 5, of which waited for: 5 -> 4; matrix products, arithmetic and copies ran while one was open for 3% -> 3% of each run, Pallas kernels for 0% -> 0%
where the time goes in v1:
time: 429 us; the launch traced here: 428 us
  waiting for transfers between devices  274 us (64%)
  blocking collectives  119 us (28%)
  between operations  14.1 us (3%)
  matrix products  10.8 us (3%)
  local copies, waits for them, and re-layouts  7.12 us (2%)
    psum x1, waiting for transfers between devices, body(): diagonal_all = lax.psum(partial_diag, ('prow', 'pcol'))  130 us
    reduce_scatter x1, waiting for transfers between devices, body(): lax.psum_scatter(cross.astype(jnp.bfloat16), 'prow', scatter_dimension=0,...  60.5 us
    reduce_scatter x1, waiting for transfers between devices, body(): lax.psum_scatter(quadratic_two.astype(jnp.bfloat16), 'prow', scatter_dime...  57.2 us
    all_gather x1, blocking collectives, body(): spread_all = lax.all_gather(spread_one, 'prow', axis=0, tiled=True)  31.9 us
    all_gather x1, blocking collectives, body(): lax.all_gather(spread_two, 'prow', axis=0, tiled=True)  31.5 us
    all_gather x1, blocking collectives, body(): lax.all_gather(scaled_parent, 'prow', axis=0, tiled=True)  26.4 us
    psum x1, waiting for transfers between devices, body(): lax.psum(partial_two.astype(jnp.bfloat16), 'pcol').astype(jnp.float32)  26.2 us
    psum x1, blocking collectives, body(): lax.psum(quadratic_part.astype(jnp.bfloat16), 'pcol').astype(jnp.float32)  10.8 us
  transfers between devices with their start and end apart: 5, of which 4 were waited for; matrix products, arithmetic and copies ran while one was open for 3% of the time, Pallas kernels for 0%

profile of v1, /device:TPU:0, one launch (start us, length us, event | category | flops | bytes accessed | tf_op | source)
XLA Modules:
  0.0 428.4 jit_solution(16851071466511964490)
XLA Ops:
  7.2 1.1 fusion.10
  8.4 7.2 %all-gather = bf16[8,128,128]{2,1,0:T(8,128)(2,1)S(1)} all-gather(bf16[2,128,128]{2,1,0:T(8,128)(2,1)S(1)} %copy.72), channel_id=2, replica_groups=mesh['prow'=8,'pcol'=4] {'pcol'}, dimensions={0}, use_global_device_ids=true | all-gather | bytes 327680 | tf_op jit(solution)/shard_map/all_gather | solution.py:44
  16.0 31.9 %all-gather.1 = bf16[16,128,128]{2,1,0:T(8,128)(2,1)S(1)} all-gather(bf16[2,128,128]{2,1,0:T(8,128)(2,1)S(1)} %copy.74), channel_id=3, replica_groups=mesh['prow'=8,'pcol'=4] {'prow'}, dimensions={0}, use_global_device_ids=true | all-gather | bytes 589824 | tf_op jit(solution)/shard_map/all_gather | solution.py:50
  47.9 1.1 fusion.7
  50.5 5.8 %all-gather.2 = bf16[8,128,128]{2,1,0:T(8,128)(2,1)S(1)} all-gather(bf16[2,128,128]{2,1,0:T(8,128)(2,1)S(1)} %copy.79), channel_id=4, replica_groups=mesh['prow'=8,'pcol'=4] {'pcol'}, dimensions={0}, use_global_device_ids=true | all-gather | bytes 327680 | tf_op jit(solution)/shard_map/all_gather | solution.py:81
  56.6 31.5 %all-gather.3 = bf16[16,128,128]{2,1,0:T(8,128)(2,1)S(1)} all-gather(bf16[2,128,128]{2,1,0:T(8,128)(2,1)S(1)} %copy.81), channel_id=5, replica_groups=mesh['prow'=8,'pcol'=4] {'prow'}, dimensions={0}, use_global_device_ids=true | all-gather | bytes 589824 | tf_op jit(solution)/shard_map/all_gather | solution.py:98
  88.3 26.4 %all-gather.4 = bf16[1024,128]{0,1:T(8,128)(2,1)S(1)} all-gather(bf16[128,128]{0,1:T(8,128)(2,1)S(1)} %bitcast.158), channel_id=6, replica_groups=mesh['prow'=8,'pcol'=4] {'prow'}, dimensions={0}, use_global_device_ids=true | all-gather | bytes 294912 | tf_op jit(solution)/shard_map/all_gather | solution.py:99
  115.4 1.1 fusion.110
  117.2 0.9 fusion.9
  118.2 0.9 copy-done.1
  121.3 0.9 copy.92
  122.2 1.0 fusion.6
  123.3 26.2 %all-reduce.8.cloned.1.call-done = bf16[1,8,128,128]{2,3,1,0:T(8,128)(2,1)} async-done(((bf16[1,8,128,128]{2,3,1,0:T(8,128)(2,1)}), bf16[1,8,128,128]{2,3,1,0:T(8,128)(2,1)}) %all-reduce.8.cloned.1.call-update) | async-done | bytes 262160 | tf_op jit(solution)/shard_map/psum | solution.py:114
  149.5 1.1 fusion.21
  150.6 0.9 copy.93
  151.8 1.0 fusion.3
  152.8 129.8 %all-reduce.6.cloned.1.call-done = f32[8,128,128]{2,1,0:T(8,128)} async-done(((f32[8,128,128]{2,1,0:T(8,128)}), f32[8,128,128]{2,1,0:T(8,128)}) %all-reduce.6.cloned.1.call-update) | async-done | bytes 524304 | tf_op jit(solution)/shard_map/psum | solution.py:71
  282.6 1.8 fusion.23
  284.5 1.5 constant_dynamic-slice_fusion.3
  285.9 60.5 %reduce-scatter.3.cloned.1.call-done = bf16[1,128,128]{2,1,0:T(8,128)(2,1)} async-done(((bf16[8,128,128]{2,1,0:T(8,128)(2,1)}), bf16[1,128,128]{2,1,0:T(8,128)(2,1)}) %reduce-scatter.3.cloned.1.call-update) | async-done | bytes 32784 | tf_op jit(solution)/shard_map/reduce_scatter | solution.py:127
  346.4 5.6 %all-gather.5 = bf16[4,128,128]{2,1,0:T(8,128)(2,1)S(1)} all-gather(bf16[1,128,128]{2,1,0:T(8,128)(2,1)} %reduce-scatter.3.cloned.1.call-done), channel_id=7, replica_groups=mesh['prow'=8,'pcol'=4] {'pcol'}, dimensions={0}, use_global_device_ids=true | all-gather | bytes 163840 | tf_op jit(solution)/shard_map/all_gather | solution.py:135
  353.1 57.2 %reduce-scatter.5.cloned.1.call-done = bf16[1,128,128]{2,1,0:T(8,128)(2,1)} async-done(((bf16[8,128,128]{2,1,0:T(8,128)(2,1)}), bf16[1,128,128]{2,1,0:T(8,128)(2,1)}) %reduce-scatter.5.cloned.1.call-update) | async-done | bytes 32784 | tf_op jit(solution)/shard_map/reduce_scatter | solution.py:130
  410.3 10.8 %psum.31 = bf16[1,128,128]{2,1,0:T(8,128)(2,1)S(1)} all-reduce(bf16[1,128,128]{2,1,0:T(8,128)(2,1)} %reduce-scatter.5.cloned.1.call-done), channel_id=1, replica_groups=mesh['prow'=8,'pcol'=4] {'pcol'}, use_global_device_ids=true, to_apply=%region_9.10 | all-reduce | flops 16384 | bytes 65536 | tf_op jit(solution)/shard_map/psum | solution.py:136
  421.1 0.8 fusion.14
  (63 shorter events, 7.6 us)
Async XLA Ops:
  7.2 40.7 %copy-start = (bf16[1,2,128,128]{3,2,1,0:T(8,128)(2,1)S(1)}, bf16[1,2,128,128]{3,2,1,0:T(8,128)(2,1)}, u32[]{:S(2)}) copy-start(bf16[1,2,128,128]{3,2,1,0:T(8,128)(2,1)} %param.9) | copy-start | bytes 196612
  7.2 108.2 %all-reduce.4.cloned.1.call-start = ((), (), s32[]{:S(2)}) async-start(), calls=%async_computation.2 | async-start | bytes 524288 | tf_op jit(solution)/shard_map/psum | solution.py:54
  8.4 7.2 %copy-start.8 = (s32[8,8]{1,0:T(8,128)S(1)}, s32[8,8]{1,0:T(8,128)}, u32[]{:S(2)}) copy-start(s32[8,8]{1,0:T(8,128)} %param.12) | copy-start | bytes 772
  48.9 100.5 %all-reduce.8.cloned.1.call-start = ((), (), s32[]{:S(2)}) async-start(), calls=%async_computation.4 | async-start | bytes 524288 | tf_op jit(solution)/shard_map/psum | solution.py:114
  49.1 0.7 copy-start.10
  49.1 0.8 copy-start.9
  49.1 1.0 copy-start.6
  49.4 0.8 copy-start.4
  56.6 31.5 %copy-start.7 = (bf16[1,128,128]{2,1,0:T(8,128)(2,1)S(1)}, bf16[1,128,128]{2,1,0:T(8,128)(2,1)}, u32[]{:S(2)}) copy-start(bf16[1,128,128]{2,1,0:T(8,128)(2,1)} %param.14) | copy-start | bytes 98308
  118.1 0.9 copy-start.1
  118.1 164.5 %all-reduce.6.cloned.1.call-start = ((), (), s32[]{:S(2)}) async-start(), calls=%async_computation.3 | async-start | bytes 1048576 | tf_op jit(solution)/shard_map/psum | solution.py:71
  119.4 0.8 copy-start.5
  120.3 0.8 copy-start.2
  121.1 225.3 %reduce-scatter.3.cloned.1.call-start = ((), (), s32[]{:S(2)}) async-start(), calls=%async_computation.5 | async-start | bytes 294912 | tf_op jit(solution)/shard_map/reduce_scatter | solution.py:127
  123.2 287.1 %reduce-scatter.5.cloned.1.call-start = ((), (), s32[]{:S(2)}) async-start(), calls=%async_computation.6 | async-start | bytes 294912 | tf_op jit(solution)/shard_map/reduce_scatter | solution.py:130
  150.5 1.0 copy-start.3
Sparse Core Ops, SparseCore 0:
  49.1 32.7 all-reduce.3
  118.3 31.1 all-reduce.7
  154.8 127.7 all-reduce.5
  286.1 60.2 reduce-scatter.2
  350.0 60.2 reduce-scatter.4
